TPU v7x, 128 devices: a whole 4x4x4 slice. The times are simulated.
128 devices in a mesh: seq: 16 (over x, y), exp: 8 (over z, core).
Axes of the slice: x: 4, y: 4, z: 4, core: 2. Of those that a mesh axis runs over, the one named last changes fastest.
Arguments:
- upstream: bfloat16 [8192, 6144], P(('seq', 'exp')), may hold values from -6 to 6
- out_weight: bfloat16 [4096, 6144], P('exp'), may hold values from -0.078125 to 0.078125
- queries: bfloat16 [8192, 4096], P('seq', 'exp'), may hold values from -6 to 6
- keys: bfloat16 [8192, 4096], P('seq', 'exp'), may hold values from -6 to 6
- values: bfloat16 [8192, 4096], P('seq', 'exp'), may hold values from -6 to 6
- log_decay: float32 [32, 8192], P('exp', 'seq'), may hold values from -0.8 to 0, as said below
- expert_ids: int32 [8192, 2], P(('seq', 'exp')), may hold values from 0 to 15, all different within a row; in each aligned block of 64 rows (0 to 63, 64 to 127, ...) at most 9 rows name the same one
- gate_probs: float32 [8192, 2], P(('seq', 'exp')), may hold values from 0.05 to 0.95
- activations: bfloat16 [16, 4608, 1152], P('exp', 'seq'), may hold values from -1.5 to 1.5
Outputs:
- d_queries: bfloat16 [8192, 4096], P('seq', 'exp')
- d_keys: bfloat16 [8192, 4096], P('seq', 'exp')
- d_values: bfloat16 [8192, 4096], P('seq', 'exp')
- d_down: bfloat16 [16, 4608, 6144], P('exp', 'seq')
Inputs may be any that keep to these rules, and one draw needn't show every extreme that they name: `expert_ids`: each row names two different experts. In every block of 64 rows no expert is named more than 9 times, and in every draw some block names some expert exactly 9 times. `log_decay`: negative at every position.
All inputs are finite; a program needn't handle non-finite values.
Results may differ from a plain program's by a relative error of at most 0.005.
Values may be sent and summed in bfloat16 or wider, within the bound.
A program may use at most 192 MiB of HBM per device.

v0:
```python
import math

import jax
import jax.numpy as jnp
from jax import lax
from jax.sharding import PartitionSpec as P

HEAD = 128
EXPERTS = 16


HIGH = lax.Precision.HIGHEST


def prefix(value, axis, join, neutral, backward):
    count, mine = (lax.axis_size(axis), lax.axis_index(axis))
    pieces = jax.tree.map(lambda part: lax.all_gather(part, axis), value)
    if backward:
        pieces = jax.tree.map(lambda part: part[::-1], pieces)
        mine = count - 1 - mine
    so_far = jax.tree.map(
        lambda part, zero: jnp.full_like(part, 0) + jnp.asarray(zero, part.dtype), value, neutral
    )

    def hop(position, so_far):
        longer = join(so_far, jax.tree.map(lambda part: part[position], pieces))
        return jax.tree.map(lambda new, old: jnp.where(position < mine, new, old), longer, so_far)

    return lax.fori_loop(0, count - 1, hop, so_far)


def block_terms(
    raw_query,
    raw_key,
    raw_value,
    raw_grad,
    query_heads,
    key_heads,
    value_heads,
    grad_heads,
    cumulative,
    lead,
    tail,
    state_in,
    adjoint_in,
):
    length = cumulative.shape[1]
    position = jnp.arange(length)
    lower = position[:, None] >= position[None, :]
    spread = cumulative[:, :, None] - cumulative[:, None, :]
    weights = jnp.where(lower[None], jnp.exp(jnp.minimum(spread, 0.0)), 0.0)
    mixed = (
        jnp.einsum("thf,shf->hts", raw_grad, raw_value, preferred_element_type=jnp.float32)
        * weights
    )
    paired = (
        jnp.einsum("the,she->hts", raw_query, raw_key, preferred_element_type=jnp.float32) * weights
    )
    d_query = jnp.einsum("hts,she->the", mixed, key_heads, precision=HIGH) + lead * jnp.einsum(
        "thf,hef->the", grad_heads, state_in, precision=HIGH
    )
    d_key = jnp.einsum("hts,the->she", mixed, query_heads, precision=HIGH) + tail * jnp.einsum(
        "shf,hef->she", value_heads, adjoint_in, precision=HIGH
    )
    d_value = jnp.einsum("hts,thf->shf", paired, grad_heads, precision=HIGH) + tail * jnp.einsum(
        "she,hef->shf", key_heads, adjoint_in, precision=HIGH
    )
    return (d_query, d_key, d_value)


def forward_join(earlier, later):
    return (earlier[0] * later[0], later[0][:, None, None] * earlier[1] + later[1])


def reverse_join(earlier, later):
    return (earlier[0] * later[0], later[1] + later[0][:, None, None] * earlier[1])


def shards(
    upstream, out_weight, queries, keys, values, log_decay, expert_ids, gate_probs, activations
):
    seq_count = lax.axis_size("seq")
    exp_count = lax.axis_size("exp")
    rows_here = queries.shape[0]
    heads_here = queries.shape[1] // HEAD
    scale = 1.0 / math.sqrt(HEAD * rows_here * seq_count)
    most = activations.shape[2] // (seq_count * exp_count)
    model_width = upstream.shape[1]
    grad_out = jnp.einsum(
        "td,fd->tf",
        lax.all_gather(upstream, "exp", axis=0, tiled=True),
        out_weight,
        preferred_element_type=jnp.float32,
    ).astype(jnp.bfloat16)
    flat_experts = expert_ids.reshape(-1)
    onehot = (flat_experts[:, None] == jnp.arange(EXPERTS, dtype=jnp.int32)[None, :]).astype(
        jnp.int32
    )
    earlier = jnp.cumsum(onehot, axis=0) - onehot
    rank = jnp.sum(earlier * onehot, axis=1)
    slot = flat_experts * most + rank
    routed = (
        (gate_probs[:, :, None] * upstream[:, None, :].astype(jnp.float32))
        .astype(jnp.bfloat16)
        .reshape(-1, model_width)
    )
    select = (jnp.arange(EXPERTS * most, dtype=jnp.int32)[:, None] == slot[None, :]).astype(
        jnp.bfloat16
    )
    outgoing = (
        jnp.dot(select, routed, preferred_element_type=jnp.float32)
        .astype(jnp.bfloat16)
        .reshape(EXPERTS, most, model_width)
    )
    incoming = lax.all_to_all(outgoing, "exp", split_axis=0, concat_axis=1, tiled=True)

    def split_raw(block):
        return block.reshape(rows_here, heads_here, HEAD)

    raw_query = split_raw(queries)
    raw_key = split_raw(keys)
    raw_value = split_raw(values)
    raw_grad = split_raw(grad_out)
    query_heads = raw_query.astype(jnp.float32)
    key_heads = raw_key.astype(jnp.float32)
    value_heads = raw_value.astype(jnp.float32)
    grad_heads = raw_grad.astype(jnp.float32)
    cumulative = jnp.cumsum(log_decay, axis=1)
    totals = cumulative[:, -1]
    lead = jnp.exp(cumulative).T[:, :, None]
    tail = jnp.exp(cumulative[:, -1:] - cumulative).T[:, :, None]
    kv_sum = jnp.einsum("she,shf->hef", key_heads * tail, value_heads, precision=HIGH)
    qo_sum = jnp.einsum("the,thf->hef", query_heads * lead, grad_heads, precision=HIGH)
    head_decay = jnp.exp(totals)
    identity_pair = (
        jnp.ones((heads_here,), jnp.float32),
        jnp.zeros((heads_here, HEAD, HEAD), jnp.float32),
    )
    state_in = prefix((head_decay, kv_sum), "seq", forward_join, identity_pair, False)[1]
    adjoint_in = prefix((head_decay, qo_sum), "seq", reverse_join, identity_pair, True)[1]
    d_query, d_key, d_value = block_terms(
        raw_query,
        raw_key,
        raw_value,
        raw_grad,
        query_heads,
        key_heads,
        value_heads,
        grad_heads,
        cumulative,
        lead,
        tail,
        state_in,
        adjoint_in,
    )
    width = heads_here * HEAD
    d_queries = (scale * d_query).reshape(rows_here, width).astype(jnp.bfloat16)
    d_keys = (scale * d_key).reshape(rows_here, width).astype(jnp.bfloat16)
    d_values = (scale * d_value).reshape(rows_here, width).astype(jnp.bfloat16)
    gathered = lax.all_gather(incoming, "seq", axis=1, tiled=True)
    d_down = jnp.einsum("ehs,esd->ehd", activations, gathered, preferred_element_type=jnp.float32)
    return (d_queries, d_keys, d_values, d_down.astype(jnp.bfloat16))


def solution(mesh):
    return jax.shard_map(
        shards,
        mesh=mesh,
        in_specs=(
            P(("seq", "exp"), None),
            P("exp", None),
            P("seq", "exp"),
            P("seq", "exp"),
            P("seq", "exp"),
            P("exp", "seq"),
            P(("seq", "exp"), None),
            P(("seq", "exp"), None),
            P("exp", "seq", None),
        ),
        out_specs=(P("seq", "exp"), P("seq", "exp"), P("seq", "exp"), P("exp", "seq", None)),
        check_vma=False,
    )
```

profile of v0, /device:TPU:0, one launch (start us, length us, event | category | flops | bytes accessed | tf_op | source)
XLA Modules:
  0.0 359.5 jit_solution(13961593589067682039)
XLA Ops:
  8.7 1.2 reduce-window.6
  10.5 1.3 copy.50
  11.8 2.5 fusion.47
  14.5 1.3 copy.54
  15.7 37.6 %all-gather.8.cloned.1.call-done = bf16[512,6144]{1,0:T(8,128)(2,1)} async-done(((bf16[64,6144]{1,0:T(8,128)(2,1)}), bf16[512,6144]{1,0:T(8,128)(2,1)}) %all-gather.8.cloned.1.call-update) | async-done | bytes 6291472 | tf_op jit(solution)/shard_map/all_gather | solution.py:91
  53.4 8.0 %convolution_convert_fusion.2 = bf16[512,512]{0,1:T(8,128)(2,1)S(1)} fusion(bf16[512,6144]{1,0:T(8,128)(2,1)} %all-gather.8.cloned.1.call-done, bf16[512,6144]{1,0:T(8,128)(2,1)} %param.14), kind=kOutput, calls=%fused_computation.44 | convolution fusion | flops 3221487616 | bytes 13107200 | tf_op jit(solution)/shard_map/td,fd->tf/dot_general | solution.py:89
  62.2 1.4 fusion.44
  63.9 3.2 mul.145
  67.1 5.1 %mul.146 = f32[128,6144]{1,0:T(8,128)} reshape(f32[64,2,6144]{2,1,0:T(2,128)} %mul.145) | data formatting | bytes 6291456 | tf_op jit(solution)/shard_map/mul | solution.py:103
  72.9 2.6 convolution_convert_fusion.1
  75.5 2.1 reshape.116
  77.6 42.5 %all_to_all.18 = bf16[16,9,6144]{2,1,0:T(8,128)(2,1)S(1)} all-to-all(bf16[16,9,6144]{2,1,0:T(8,128)(2,1)} %reshape.116), channel_id=1, replica_groups=mesh['seq'=16,'exp'=8] {'exp'}, dimensions={0} | all-to-all | bytes 3538944 | tf_op jit(solution)/shard_map/all_to_all | solution.py:115
  120.1 1.9 copy.63
  122.0 1.8 copy.64
  125.4 40.8 %all-reduce = f32[64]{0:T(128)S(1)} all-reduce(f32[64]{0:T(128)S(1)} %bitcast_dynamic-update-slice_fusion), channel_id=2, replica_groups=mesh['seq'=16,'exp'=8] {'seq'}, use_global_device_ids=true, to_apply=%add | all-reduce | flops 64 | bytes 512
  167.2 2.7 fusion.64
  169.9 16.6 %while.28 = (s32[]{:T(128)}, f32[4,128,128]{2,1,0:T(8,128)S(1)}, s32[]{:T(128)}, f32[16,4]{1,0:T(8,128)S(1)}, f32[16,4,128,128]{3,2,1,0:T(8,128)}, /*index=5*/s32[]{:T(128)}, s32[]{:T(128)}) while((s32[]{:T(128)}, f32[4,128,128]{2,1,0:T(8,128)S(1)}, s32[]{:T(128)}, f32[16,4]{1,0:T(8,128)S(1)}, f32[16,4,128,128]{3,2,1,0:T(8,128)}, ...), condition=%wide.region_3.4_spmd.clone, body=%wide.region_2.3_spmd.clone.sunk | while | flops 262148 | bytes 786585 | solution.py:29
  186.5 1.9 fusion.52
  188.4 3.5 fusion.23
  191.8 1.4 fusion.41
  193.2 2.1 copy.65
  195.3 6.1 %fusion.29 = f32[512,4,128]{0,2,1:T(8,128)} fusion(bf16[512,4,128]{0,2,1:T(8,128)(2,1)S(1)} %bitcast.133, f32[4,512,512]{2,1,0:T(8,128)} %fusion.64, f32[4,512]{1,0:T(4,128)S(1)} %bitcast.141, pred[512,512]{1,0:T(8,128)(4,1)} %iota_compare_fusion), kind=kOutput, calls=%fused_computation.31 | convolution fusion | flops 1614807040 | bytes 6037504 | tf_op jit(solution)/shard_map/hts,thf->shf/dot_general | solution.py:65
  201.4 3.9 %fusion.26 = f32[512,4,128]{0,2,1:T(8,128)} fusion(bf16[512,4,128]{0,2,1:T(8,128)(2,1)S(1)} %bitcast.125, f32[4,512,512]{2,1,0:T(8,128)S(1)} %copy-done.8, f32[4,512]{1,0:T(4,128)S(1)} %bitcast.142, pred[512,512]{1,0:T(8,128)(4,1)S(1)} %copy-done.12), kind=kOutput, calls=%fused_computation.30 | convolution fusion | flops 1614807040 | bytes 6037504 | tf_op jit(solution)/shard_map/hts,the->she/dot_general | solution.py:62
  205.3 4.7 %rev.6 = f32[16,4,128,128]{3,2,1,0:T(8,128)} reverse(f32[16,4,128,128]{3,2,1,0:T(8,128)} %bitcast.134), dimensions={0} | reverse | bytes 8388608 | tf_op jit(solution)/shard_map/rev | solution.py:19
  210.0 16.8 %while.29 = (s32[]{:T(128)}, f32[4,128,128]{2,1,0:T(8,128)S(1)}, s32[]{:T(128)}, f32[16,4,128,128]{3,2,1,0:T(8,128)}, f32[16,4]{1,0:T(8,128)S(1)}, /*index=5*/s32[]{:T(128)}, s32[]{:T(128)}) while((s32[]{:T(128)}, f32[4,128,128]{2,1,0:T(8,128)S(1)}, s32[]{:T(128)}, f32[16,4,128,128]{3,2,1,0:T(8,128)}, f32[16,4]{1,0:T(8,128)S(1)}, ...), condition=%wide.region_5.6_spmd.clone, body=%wide.region_4.5_spmd.clone.sunk | while | flops 262148 | bytes 786585 | solution.py:29
  214.4 1.1 fusion.87
  215.6 1.1 fusion.87
  216.8 1.1 fusion.87
  226.8 1.9 fusion.43
  229.7 1.9 fusion.42
  232.5 99.7 %all-gather.10.cloned.1.call-done = bf16[2,1152,6144]{2,1,0:T(8,128)(2,1)} async-done(((bf16[2,72,6144]{2,1,0:T(8,128)(2,1)}), bf16[2,1152,6144]{2,1,0:T(8,128)(2,1)}) %all-gather.10.cloned.1.call-update) | async-done | bytes 28311568 | tf_op jit(solution)/shard_map/all_gather | solution.py:160
  332.3 20.7 %fusion.2 = bf16[2,288,6144]{2,1,0:T(8,128)(2,1)} fusion(bf16[2,288,1152]{2,1,0:T(8,128)(2,1)S(1)} %copy-done, bf16[2,1152,6144]{2,1,0:T(8,128)(2,1)} %all-gather.10.cloned.1.call-done), kind=kOutput, calls=%fused_computation.7 | convolution fusion | flops 8157265920 | bytes 36716544 | tf_op jit(solution)/shard_map/ehs,esd->ehd/dot_general | solution.py:161
  (125 shorter events, 36.9 us)
Async XLA Ops:
  7.2 325.1 %copy-start = (bf16[2,288,1152]{2,1,0:T(8,128)(2,1)S(1)}, bf16[2,288,1152]{2,1,0:T(8,128)(2,1)}, u32[]{:S(2)}) copy-start(bf16[2,288,1152]{2,1,0:T(8,128)(2,1)} %param.21) | copy-start | bytes 3981316
  7.2 46.2 %all-gather.8.cloned.1.call-start = ((), (), s32[]{:S(2)}) async-start(), calls=%async_computation.1 | async-start | bytes 7077888 | tf_op jit(solution)/shard_map/all_gather | solution.py:91
  7.9 162.0 %all-gather.12.cloned.1.call-start = ((), (), s32[]{:S(2)}) async-start(), calls=%async_computation.3 | async-start | bytes 4456448 | tf_op jit(solution)/shard_map/all_gather | solution.py:17
  11.7 2.7 copy-start.3
  14.4 190.9 %all-gather.14.cloned.1.call-start = ((), (), s32[]{:S(2)}) async-start(), calls=%async_computation.4 | async-start | bytes 4456448 | tf_op jit(solution)/shard_map/all_gather | solution.py:17
  15.7 45.7 %copy-start.1 = (bf16[512,512]{0,1:T(8,128)(2,1)}, bf16[512,512]{0,1:T(8,128)(2,1)S(1)}, u32[]{:S(2)}) copy-start(bf16[512,512]{0,1:T(8,128)(2,1)S(1)} %copy.54) | copy-start | bytes 1572868
  15.7 47.9 %copy-start.13 = (s32[64,2]{0,1:T(2,128)S(1)}, s32[64,2]{0,1:T(2,128)}, u32[]{:S(2)}) copy-start(s32[64,2]{0,1:T(2,128)} %param.19) | copy-start | bytes 1540
  15.7 48.2 %copy-start.9 = (bf16[64,6144]{1,0:T(8,128)(2,1)S(1)}, bf16[64,6144]{1,0:T(8,128)(2,1)}, u32[]{:S(2)}) copy-start(bf16[64,6144]{1,0:T(8,128)(2,1)} %param.13) | copy-start | bytes 2359300
  61.4 0.8 copy-start.5
  63.6 268.7 %all-gather.10.cloned.1.call-start = ((), (), s32[]{:S(2)}) async-start(), calls=%async_computation.2 | async-start | bytes 30081024 | tf_op jit(solution)/shard_map/all_gather | solution.py:160
  63.9 8.3 %copy-start.14 = (f32[64,2]{0,1:T(2,128)S(1)}, f32[64,2]{0,1:T(2,128)}, u32[]{:S(2)}) copy-start(f32[64,2]{0,1:T(2,128)} %param.20) | copy-start | bytes 1540
  120.0 3.8 %copy-start.15 = (u32[128]{0:T(128)S(1)}, u32[128]{0:T(128)}, u32[]{:S(2)}) copy-start(u32[128]{0:T(128)} %constant.76) | copy-start | bytes 1540
  120.0 47.1 %copy-start.2 = (bf16[512,512]{0,1:T(8,128)(2,1)S(1)}, bf16[512,512]{0,1:T(8,128)(2,1)}, u32[]{:S(2)}) copy-start(bf16[512,512]{0,1:T(8,128)(2,1)} %copy-done.1) | copy-start | bytes 1572868
  120.1 47.1 %copy-start.4 = (bf16[512,512]{0,1:T(8,128)(2,1)S(1)}, bf16[512,512]{0,1:T(8,128)(2,1)}, u32[]{:S(2)}) copy-start(bf16[512,512]{0,1:T(8,128)(2,1)} %copy-done.3) | copy-start | bytes 1572868
  167.2 19.3 %copy-start.6 = (bf16[512,512]{0,1:T(8,128)(2,1)S(1)}, bf16[512,512]{0,1:T(8,128)(2,1)}, u32[]{:S(2)}) copy-start(bf16[512,512]{0,1:T(8,128)(2,1)} %copy-done.5) | copy-start | bytes 1572868
  186.5 1.9 copy-start.11
  188.3 4.9 %copy-start.7 = (f32[4,512,512]{2,1,0:T(8,128)}, f32[4,512,512]{2,1,0:T(8,128)S(1)}, u32[]{:S(2)}) copy-start(f32[4,512,512]{2,1,0:T(8,128)S(1)} %fusion.52) | copy-start | bytes 12582916
  193.2 8.2 %copy-start.12 = (pred[512,512]{1,0:T(8,128)(4,1)S(1)}, pred[512,512]{1,0:T(8,128)(4,1)}, u32[]{:S(2)}) copy-start(pred[512,512]{1,0:T(8,128)(4,1)} %iota_compare_fusion) | copy-start | bytes 786436
  195.3 6.1 %copy-start.8 = (f32[4,512,512]{2,1,0:T(8,128)S(1)}, f32[4,512,512]{2,1,0:T(8,128)}, u32[]{:S(2)}) copy-start(f32[4,512,512]{2,1,0:T(8,128)} %copy-done.7) | copy-start | bytes 12582916
  210.0 19.7 %copy-start.10 = (bf16[512,512]{1,0:T(8,128)(2,1)S(1)}, bf16[512,512]{1,0:T(8,128)(2,1)}, u32[]{:S(2)}) copy-start(bf16[512,512]{1,0:T(8,128)(2,1)} %param.17) | copy-start | bytes 1572868
Sparse Core Ops, SparseCore 0:
  9.7 43.6 all-gather.7
  55.5 51.3 all-gather.11
  109.0 51.4 all-gather.13
  162.6 169.6 all-gather.9
where the time goes:
time: 362 us; the launch traced here: 359 us
  waiting for transfers between devices  138 us (38%)
  blocking collectives  83.3 us (23%)
  matrix products  58.3 us (16%)
  other arithmetic  34.9 us (10%)
  local copies, waits for them, and re-layouts  29.1 us (8%)
  between operations  14.7 us (4%)
    all_gather x1, waiting for transfers between devices, shards(): gathered = lax.all_gather(incoming, 'seq', axis=1, tiled=True)  99.7 us
    all_to_all x1, blocking collectives, shards(): lax.all_to_all(outgoing, 'exp', split_axis=0, concat_axis=1, tiled=True)  42.5 us
    unnamed x1, blocking collectives  40.8 us
    all_gather x1, waiting for transfers between devices, shards(): lax.all_gather(upstream, 'exp', axis=0, tiled=True)  37.6 us
    select_n x30, other arithmetic, hop(): jnp.where(position < mine, new, old)  32.1 us
    dot_general x1, matrix products, shards(): jnp.einsum('ehs,esd->ehd', activations, gathered, preferred_element_type=...  20.7 us
    unnamed x44, local copies, waits for them, and re-layouts  8.71 us
    mul x3, local copies, waits for them, and re-layouts, shards(): gate_probs[:, :, None] * upstream[:, None, :].astype(jnp.float32)  8.43 us
  transfers between devices with their start and end apart: 4, of which 2 were waited for; matrix products, arithmetic and copies ran while one was open for 28% of the time, Pallas kernels for 0%

commit v1 on v0

v1 whole, which is shorter than its diff:
```python
import functools
import math

import jax
import jax.numpy as jnp
from jax import lax
from jax.experimental import pallas as pl
from jax.experimental.pallas import tpu as pltpu
from jax.sharding import PartitionSpec as P

HEAD = 128
EXPERTS = 16
MOST = 9
ROWS = 144
ZCH = 4
CH = 8
F32, BF16 = jnp.float32, jnp.bfloat16


def route_kernel(
    up_ref, meta_ref, w_hbm, act_hbm, down_hbm, grad_ref,
    G, upbuf, metabuf, wbuf, actbuf, acc, stage,
    zsend, zrecv, gsend, grecv, lsem, osem,
):
    s, j = lax.axis_index("seq"), lax.axis_index("exp")
    x, y, z, core = s // 4, s % 4, j // 2, j % 2
    width = up_ref.shape[1]
    zw, gw = width // ZCH, width // CH

    def plane(xx, yy):
        return {"seq": (xx % 4) * 4 + yy % 4, "exp": j}

    def column(zz, cc):
        return {"seq": s, "exp": (zz % 4) * 2 + cc}

    zup, zdown, mate = column(z + 1, core), column(z + 3, core), column(z, 1 - core)
    barrier = pltpu.get_barrier_semaphore()
    for peer in (plane(x + 1, y), plane(x + 3, y), plane(x, y + 1), plane(x, y + 3), zup, zdown, mate):
        pl.semaphore_signal(barrier, inc=1, device_id=peer, device_id_type=pl.DeviceIdType.MESH)

    wcopy = pltpu.make_async_copy(w_hbm, wbuf, lsem.at[0])
    acopy = pltpu.make_async_copy(act_hbm, actbuf, lsem.at[1])
    wcopy.start()
    acopy.start()
    own = [pltpu.make_async_copy(meta_ref, metabuf.at[j], lsem.at[2])] + [
        pltpu.make_async_copy(up_ref.at[:, k * zw : (k + 1) * zw], upbuf.at[k, j], lsem.at[3 + k])
        for k in range(ZCH)
    ]
    for copy in own:
        copy.start()
    pl.semaphore_wait(barrier, 7)

    def remote(src, dst, ssem, rsem, dev):
        return pltpu.make_async_remote_copy(
            src_ref=src, dst_ref=dst, send_sem=ssem, recv_sem=rsem,
            device_id=dev, device_id_type=pl.DeviceIdType.MESH,
        )

    sent = []

    def zslot(item, slot):
        return metabuf.at[slot] if item == ZCH else upbuf.at[item, slot]

    def zsource(item):
        return meta_ref if item == ZCH else up_ref.at[:, item * zw : (item + 1) * zw]

    def zgo(item, n, src, slot, rn, dev):
        copy = remote(src, zslot(item, slot), zsend.at[item, n], zrecv.at[item, rn], dev)
        copy.start()
        sent.append(copy)

    def zwait(item, rn, slot):
        remote(zslot(item, slot), zslot(item, slot), zsend.at[item, 0], zrecv.at[item, rn], mate).wait_recv()

    def exps(zz, cc):
        return ((zz + 4) % 4) * 2 + cc

    for item in (ZCH, *range(ZCH)):
        zgo(item, 0, zsource(item), j, 0, zup)
        zgo(item, 1, zsource(item), j, 1, zdown)
        zgo(item, 2, zsource(item), j, 3, mate)

    def zforward(item):
        below, above, far = exps(z - 1, core), exps(z + 1, core), exps(z + 2, core)
        zwait(item, 0, below)
        if item % 2 == 0:
            zgo(item, 3, zslot(item, below), below, 2, zup)
        zgo(item, 4, zslot(item, below), below, 4, mate)
        zwait(item, 1, above)
        if item % 2 == 1:
            zgo(item, 3, zslot(item, above), above, 2, zdown)
        zgo(item, 5, zslot(item, above), above, 5, mate)

    def zfinish(item):
        far = exps(z + 2, core)
        zwait(item, 2, far)
        zgo(item, 6, zslot(item, far), far, 6, mate)
        for rn, slot in ((3, exps(z, 1 - core)), (4, exps(z - 1, 1 - core)), (5, exps(z + 1, 1 - core)), (6, exps(z + 2, 1 - core))):
            zwait(item, rn, slot)

    def ring(c):
        if c % 2 == 0:
            return x, y, (lambda d: plane(x + d, y)), (lambda d: plane(x, y + d))
        return y, x, (lambda d: plane(x, y + d)), (lambda d: plane(x + d, y))

    def ggo(c, n, ref, dev):
        copy = remote(ref, ref, gsend.at[c, n], grecv.at[c, n], dev)
        copy.start()
        sent.append(copy)

    def gwait(c, n, ref):
        remote(ref, ref, gsend.at[c, n], grecv.at[c, n], mate).wait_recv()

    def slab(c, a, b):
        return G.at[c, b * 4 + (a + 4) % 4]

    def group(c, b):
        return G.at[c, pl.ds(((b + 4) % 4) * 4, 4)]

    def turn(c):
        return (c // 2) % 2 == 0

    def stage1(c):
        a, b, na, _ = ring(c)
        ggo(c, 0, slab(c, a, b), na(1))
        ggo(c, 1, slab(c, a, b), na(3))

    def stage2(c):
        a, b, na, _ = ring(c)
        if turn(c):
            gwait(c, 0, slab(c, a - 1, b))
            ggo(c, 2, slab(c, a - 1, b), na(1))
            gwait(c, 1, slab(c, a + 1, b))
        else:
            gwait(c, 1, slab(c, a + 1, b))
            ggo(c, 2, slab(c, a + 1, b), na(3))
            gwait(c, 0, slab(c, a - 1, b))

    def stage3(c):
        a, b, _, nb = ring(c)
        gwait(c, 2, slab(c, a + 2, b))
        ggo(c, 3, group(c, b), nb(1))
        ggo(c, 4, group(c, b), nb(3))

    def stage4(c):
        a, b, _, nb = ring(c)
        if turn(c):
            gwait(c, 3, group(c, b - 1))
            ggo(c, 5, group(c, b - 1), nb(1))
            gwait(c, 4, group(c, b + 1))
        else:
            gwait(c, 4, group(c, b + 1))
            ggo(c, 5, group(c, b + 1), nb(3))
            gwait(c, 3, group(c, b - 1))

    outs = []

    def stage5(c):
        a, b, _, _ = ring(c)
        gwait(c, 5, group(c, b + 2))
        if c >= 2:
            outs[c - 2].wait()
        for e in range(2):
            order = [(q % 4) * 4 + q // 4 if c % 2 == 0 else q for q in range(16)]
            rows = jnp.concatenate([G[c, q, e * 72 : (e + 1) * 72, :] for q in order], axis=0)
            stage[c % 2, e] = jnp.dot(actbuf[e], rows, preferred_element_type=F32).astype(BF16)
        out = pltpu.make_async_copy(stage.at[c % 2], down_hbm.at[:, :, c * gw : (c + 1) * gw], osem.at[c % 2])
        out.start()
        outs.append(out)

    for copy in own:
        copy.wait()
    zforward(ZCH)
    zfinish(ZCH)
    row = lax.broadcasted_iota(jnp.int32, (ROWS, 64), 0)
    local = row % 72
    base = (row // 72 + 2 * j) * MOST + local % MOST
    block_of = local // MOST
    picks, gates = [], []
    for t in range(8):
        table = metabuf[t]
        code0, code1 = table[0:1, 0:64], table[1:2, 0:64]
        gate0, gate1 = table[2:3, 0:64], table[3:4, 0:64]
        want = jnp.where(block_of == t, base, -1).astype(F32)
        hit0, hit1 = want == code0, want == code1
        picks.append(jnp.where(hit0 | hit1, 1.0, 0.0))
        gates.append(jnp.sum(jnp.where(hit0, gate0, 0.0) + jnp.where(hit1, gate1, 0.0), axis=1, keepdims=True))
    pick = jnp.concatenate(picks, axis=1).astype(BF16)
    gate = sum(gates)

    def select(c):
        k, off = c // (CH // ZCH), (c % (CH // ZCH)) * gw
        tokens = upbuf[k, :, :, off : off + gw].reshape(512, gw)
        a, b, _, _ = ring(c)
        rows = jnp.dot(pick, tokens, preferred_element_type=F32)
        G[c, b * 4 + a] = (rows * gate).astype(BF16)
        part = lax.dot_general(
            tokens, wbuf[:, c * gw : (c + 1) * gw], (((1,), (1,)), ((), ())), preferred_element_type=F32
        )
        if c == 0:
            acc[...] = part
        else:
            acc[...] += part
        stage1(c)

    per = CH // ZCH
    zforward(0)
    for k in range(ZCH):
        zfinish(k)
        if k + 1 < ZCH:
            zforward(k + 1)
        if k == 0:
            wcopy.wait()
        for c in range(per * k, per * k + per):
            select(c)
        if k >= 1:
            for c in range(per * (k - 1), per * k):
                stage2(c)
            for c in range(per * (k - 1), per * k):
                stage3(c)
    grad_ref[...] = acc[...].astype(BF16)
    for c in range(per * (ZCH - 1), CH):
        stage2(c)
    for c in range(per * (ZCH - 1), CH):
        stage3(c)
    acopy.wait()
    for c in range(CH + 1):
        if c < CH:
            stage4(c)
        if c >= 1:
            stage5(c - 1)
    outs[CH - 2].wait()
    outs[CH - 1].wait()
    for copy in sent:
        copy.wait_send()


def route(upstream, meta, out_weight, activations):
    width = upstream.shape[1]
    gw, zw = width // CH, width // ZCH
    return pl.pallas_call(
        route_kernel,
        out_shape=(
            jax.ShapeDtypeStruct((2, 288, width), BF16),
            jax.ShapeDtypeStruct((512, 512), BF16),
        ),
        in_specs=[
            pl.BlockSpec(memory_space=pltpu.VMEM),
            pl.BlockSpec(memory_space=pltpu.VMEM),
            pl.BlockSpec(memory_space=pl.ANY),
            pl.BlockSpec(memory_space=pl.ANY),
        ],
        out_specs=(pl.BlockSpec(memory_space=pl.ANY), pl.BlockSpec(memory_space=pltpu.VMEM)),
        scratch_shapes=[
            pltpu.VMEM((CH, 16, ROWS, gw), BF16),
            pltpu.VMEM((ZCH, 8, 64, zw), BF16),
            pltpu.VMEM((8, 8, 128), F32),
            pltpu.VMEM((512, width), BF16),
            pltpu.VMEM((2, 288, 1152), BF16),
            pltpu.VMEM((512, 512), F32),
            pltpu.VMEM((2, 2, 288, gw), BF16),
            pltpu.SemaphoreType.DMA((ZCH + 1, 7)),
            pltpu.SemaphoreType.DMA((ZCH + 1, 7)),
            pltpu.SemaphoreType.DMA((CH, 6)),
            pltpu.SemaphoreType.DMA((CH, 6)),
            pltpu.SemaphoreType.DMA((3 + ZCH,)),
            pltpu.SemaphoreType.DMA((2,)),
        ],
        compiler_params=pltpu.CompilerParams(
            collective_id=0, has_side_effects=True, vmem_limit_bytes=64000 * 1024
        ),
        name="route",
    )(upstream, meta, out_weight, activations)


def scan_states(decay, value, backward):
    count, mine = lax.axis_size("seq"), lax.axis_index("seq")
    if backward:
        mine = count - 1 - mine

    def shift(part, d):
        pairs = [(i + d, i) if backward else (i, i + d) for i in range(count - d)]
        return lax.ppermute(part, "seq", pairs)

    factor, value = shift(decay, 1), shift(value, 1)
    factor = jnp.where(mine >= 1, factor, 1.0)
    d = 1
    while d < count - 1:
        other_f, other_v = shift(factor, d), shift(value, d)
        here = mine >= d
        value = value + jnp.where(here, factor[:, None, None] * other_v, 0.0)
        factor = factor * jnp.where(here, other_f, 1.0)
        d *= 2
    return value


def shards(
    upstream, out_weight, queries, keys, values, log_decay, expert_ids, gate_probs, activations
):
    rows_here = queries.shape[0]
    heads_here = queries.shape[1] // HEAD
    scale = 1.0 / math.sqrt(HEAD * rows_here * lax.axis_size("seq"))
    flat = expert_ids.reshape(-1)
    onehot = (flat[:, None] == jnp.arange(EXPERTS, dtype=jnp.int32)[None, :]).astype(F32)
    place = jnp.arange(flat.shape[0])
    before = (place[:, None] > place[None, :]).astype(F32)
    earlier = jnp.dot(before, onehot, preferred_element_type=F32)
    rank = jnp.sum(earlier * onehot, axis=1)
    code = (flat.astype(F32) * MOST + rank).reshape(-1, 2)
    meta = jnp.concatenate([code.T, gate_probs.T], axis=0)
    meta = jnp.pad(meta, ((0, 4), (0, 64)))

    d_down, grad_out = route(upstream, meta, out_weight, activations)

    def split(block):
        return block.reshape(rows_here, heads_here, HEAD).transpose(1, 0, 2)

    q, k, v, o = split(queries), split(keys), split(values), split(grad_out)
    cumulative = jnp.cumsum(log_decay, axis=1)
    lead = jnp.exp(cumulative)[:, :, None]
    tail = jnp.exp(cumulative[:, -1:] - cumulative)[:, :, None]
    decay = jnp.exp(cumulative[:, -1])

    def dot(spec, a, b):
        return jnp.einsum(spec, a, b, preferred_element_type=F32)

    kv_sum = dot("hse,hsf->hef", (k * tail).astype(BF16), v)
    qo_sum = dot("hte,htf->hef", (q * lead).astype(BF16), o)
    state_in = scan_states(decay, kv_sum, False).astype(BF16)
    adjoint_in = scan_states(decay, qo_sum, True).astype(BF16)
    position = jnp.arange(rows_here)
    lower = position[:, None] >= position[None, :]
    spread = cumulative[:, :, None] - cumulative[:, None, :]
    weights = jnp.where(lower[None], jnp.exp(jnp.minimum(spread, 0.0)), 0.0)
    mixed = (dot("htf,hsf->hts", o, v) * weights).astype(BF16)
    paired = (dot("hte,hse->hts", q, k) * weights).astype(BF16)
    d_query = dot("hts,hse->hte", mixed, k) + lead * dot("htf,hef->hte", o, state_in)
    d_key = dot("hts,hte->hse", mixed, q) + tail * dot("hsf,hef->hse", v, adjoint_in)
    d_value = dot("hts,htf->hsf", paired, o) + tail * dot("hse,hef->hsf", k, adjoint_in)

    def join(part):
        return (scale * part).astype(BF16).transpose(1, 0, 2).reshape(rows_here, -1)

    return (join(d_query), join(d_key), join(d_value), d_down)


def solution(mesh):
    return jax.shard_map(
        shards,
        mesh=mesh,
        in_specs=(
            P(("seq", "exp"), None),
            P("exp", None),
            P("seq", "exp"),
            P("seq", "exp"),
            P("seq", "exp"),
            P("exp", "seq"),
            P(("seq", "exp"), None),
            P(("seq", "exp"), None),
            P("exp", "seq", None),
        ),
        out_specs=(P("seq", "exp"), P("seq", "exp"), P("seq", "exp"), P("exp", "seq", None)),
        check_vma=False,
    )
```

time: 362 us -> 355 us (0.981)
  Pallas kernels: 0 us -> 244 us
  waiting for transfers between devices: 138 us -> 4.31 us
  blocking collectives: 83.3 us -> 0 us
  starting transfers between devices: 0.16 us -> 66.5 us
  matrix products: 58.3 us -> 14.2 us
  other arithmetic: 34.9 us -> 5.9 us
  between operations: 14.7 us -> 1.08 us
  local copies, waits for them, and re-layouts: 29.1 us -> 16.7 us
    pallas_call x0 -> x1, Pallas kernels: none -> 244 us  [route(): pl.pallas_call(route_kernel, out_shape=(jax.ShapeDtypeStruct((2, 288, wid...]
    all_gather x4 -> x0, waiting for transfers between devices: 137 us -> none  [the longest x1 99.7 us: shards(): gathered = lax.all_gather(incoming, 'seq', axis=1, tiled=True)]
    ppermute x0 -> x18, starting transfers between devices: none -> 66.5 us  [shift(): return lax.ppermute(part, 'seq', pairs)]
    dot_general x13 -> x10, matrix products: 58.3 us -> 14.2 us  [the longest x9 14.1 us: dot(): return jnp.einsum(spec, a, b, preferred_element_type=F32)]
    all_to_all x1 -> x0, blocking collectives: 42.5 us -> none  [shards(): lax.all_to_all(outgoing, 'exp', split_axis=0, concat_axis=1, tiled=True)]
    unnamed x1 -> x0, blocking collectives: 40.8 us -> none
    select_n x30 -> x2, other arithmetic: 32.1 us -> 0.01 us  [scan_states(): factor = jnp.where(mine >= 1, factor, 1.0)]
    mul x33 -> x0, local copies, waits for them, and re-layouts: 8.7 us -> none  [the longest x3 8.43 us: shards(): gate_probs[:, :, None] * upstream[:, None, :].astype(jnp.float32)]
  transfers between devices with their start and end apart: 4 -> 18, of which waited for: 2 -> 2; matrix products, arithmetic and copies ran while one was open for 28% -> 7% of each run, Pallas kernels for 0% -> 69%
where the time goes in v1:
time: 355 us; the launch traced here: 353 us
  Pallas kernels  244 us (69%)
  starting transfers between devices  66.5 us (19%)
  local copies, waits for them, and re-layouts  16.7 us (5%)
  matrix products  14.2 us (4%)
  other arithmetic  5.9 us (2%)
  waiting for transfers between devices  4.31 us (1%)
    pallas_call x1, Pallas kernels, route(): pl.pallas_call(route_kernel, out_shape=(jax.ShapeDtypeStruct((2, 288, wid...  244 us
    ppermute x18, starting transfers between devices, shift(): return lax.ppermute(part, 'seq', pairs)  66.5 us
    dot_general x9, matrix products, dot(): return jnp.einsum(spec, a, b, preferred_element_type=F32)  14.1 us
    unnamed x15, local copies, waits for them, and re-layouts  12.8 us
  transfers between devices with their start and end apart: 18, of which 2 were waited for; matrix products, arithmetic and copies ran while one was open for 7% of the time, Pallas kernels for 69%

profile of v1, /device:TPU:0, one launch (start us, length us, event | category | flops | bytes accessed | tf_op | source)
XLA Modules:
  0.0 353.2 jit_solution(13144180645903443421)
XLA Ops:
  3.2 1.3 collective-permute-start.10
  4.5 4.5 %collective-permute-start.1 = (f32[4]{0:T(128)S(1)}, f32[4]{0:T(128)S(1)}, u32[]{:S(2)}, u32[]{:S(2)}) collective-permute-start(f32[4]{0:T(128)S(1)} %bitcast_exponential_fusion), channel_id=1, source_target_pairs={{0,8},{8,16},{16,24},{24,32},{32,40},{40,48},{48,56},{56,64},{64,7... | collective-permute-start | bytes 56 | tf_op jit(solution)/shard_map/ppermute | solution.py:283
  9.2 2.5 fusion.15
  11.7 3.6 %collective-permute-start = (f32[4,128,128]{2,1,0:T(8,128)}, f32[4,128,128]{2,1,0:T(8,128)S(1)}, u32[]{:S(2)}, u32[]{:S(2)}) collective-permute-start(f32[4,128,128]{2,1,0:T(8,128)} %fusion.15), channel_id=1, source_target_pairs={{0,8},{8,16},{16,24},{24,32},{32,40},{40,48},{48,56},{56,64},{64,7... | collective-permute-start | bytes 786440 | tf_op jit(solution)/shard_map/ppermute | solution.py:283
  17.3 1.3 copy.54
  18.5 1.3 select_maximum_fusion.meta_ref
  19.8 244.5 %route.1 = (bf16[2,288,6144]{2,1,0:T(8,128)(2,1)}, bf16[512,512]{1,0:T(8,128)(2,1)}) custom-call(bf16[64,6144]{1,0:T(8,128)(2,1)} %up_ref.1, f32[8,128]{1,0:T(8,128)} %select_maximum_fusion.meta_ref, bf16[512,6144]{1,0:T(8,128)(2,1)} %w_hbm.1, bf16[2,288,1152]{2,1,0:T(8,128)(2,1)} %act_hbm.1), custom_call_target="tpu_custom_call" | custom-call | tf_op jit(solution)/shard_map/route/pallas_call | solution.py:241
  264.3 1.3 copy.51
  266.0 1.3 collective-permute-start.9
  267.4 3.9 %fusion.1 = f32[512,4,128]{0,2,1:T(8,128)} fusion(bf16[4,512,128]{1,2,0:T(8,128)(2,1)S(1)} %bitcast.130, bf16[4,512,128]{1,2,0:T(8,128)(2,1)S(1)} %bitcast.134, f32[4,512]{1,0:T(4,128)S(1)} %bitcast.142, pred[512,512]{1,0:T(8,128)(4,1)S(1)} %iota_compare_fusion, bf16[512,512]{1,0:T(8,128)(2,1)} %param.12), kind=kOutput, calls=%fused_computation.6 | convolution fusion | flops 542113792 | bytes 2891776 | tf_op jit(solution)/shard_map/hts,htf->hsf/dot_general | solution.py:325
  271.3 1.4 multiply_convert_fusion.1
  272.7 1.4 convolution_bitcast_fusion
  275.0 1.3 collective-permute-start.12
  276.3 5.2 %collective-permute-start.3 = (f32[4]{0:T(128)S(1)}, f32[4]{0:T(128)S(1)}, u32[]{:S(2)}, u32[]{:S(2)}) collective-permute-start(f32[4]{0:T(128)S(1)} %broadcast_select_fusion.7), channel_id=1, source_target_pairs={{0,8},{8,16},{16,24},{24,32},{32,40},{40,48},{48,56},{56,64},{64,7... | collective-permute-start | bytes 56 | tf_op jit(solution)/shard_map/ppermute | solution.py:283
  281.5 1.3 collective-permute-start.14
  282.8 1.3 collective-permute-start.11
  284.1 6.7 %collective-permute-start.5 = (f32[4]{0:T(128)S(1)}, f32[4]{0:T(128)S(1)}, u32[]{:S(2)}, u32[]{:S(2)}) collective-permute-start(f32[4]{0:T(128)S(1)} %fusion.31), channel_id=1, source_target_pairs={{0,16},{8,24},{16,32},{24,40},{32,48},{40,56},{48,64},{56,72},{64,... | collective-permute-start | bytes 56 | tf_op jit(solution)/shard_map/ppermute | solution.py:283
  290.9 1.4 collective-permute-start.16
  292.3 3.9 %collective-permute-start.2 = (f32[4,128,128]{2,1,0:T(8,128)S(1)}, f32[4,128,128]{2,1,0:T(8,128)S(1)}, u32[]{:S(2)}, u32[]{:S(2)}) collective-permute-start(f32[4,128,128]{2,1,0:T(8,128)S(1)} %collective-permute-done), channel_id=1, source_target_pairs={{0,8},{8,16},{16,24},{24,32},{32,40},{40,48},{48,56},{56,64},{64,7... | collective-permute-start | bytes 786440 | tf_op jit(solution)/shard_map/ppermute | solution.py:283
  297.3 1.3 collective-permute-start.13
  298.6 8.0 %collective-permute-start.7 = (f32[4]{0:T(128)S(1)}, f32[4]{0:T(128)S(1)}, u32[]{:S(2)}, u32[]{:S(2)}) collective-permute-start(f32[4]{0:T(128)S(1)} %fusion.32), channel_id=1, source_target_pairs={{0,32},{8,40},{16,48},{24,56},{32,64},{40,72},{48,80},{56,88},{64,... | collective-permute-start | bytes 56 | tf_op jit(solution)/shard_map/ppermute | solution.py:283
  306.8 9.2 %collective-permute-start.4 = (f32[4,128,128]{2,1,0:T(8,128)S(1)}, f32[4,128,128]{2,1,0:T(8,128)S(1)}, u32[]{:S(2)}, u32[]{:S(2)}) collective-permute-start(f32[4,128,128]{2,1,0:T(8,128)S(1)} %select_add_fusion.5), channel_id=1, source_target_pairs={{0,16},{8,24},{16,32},{24,40},{32,48},{40,56},{48,64},{56,72},{64,... | collective-permute-start | bytes 786440 | tf_op jit(solution)/shard_map/ppermute | solution.py:283
  316.1 1.3 collective-permute-start.15
  317.4 2.4 collective-permute-done.4
  319.9 6.6 %collective-permute-start.6 = (f32[4,128,128]{2,1,0:T(8,128)S(1)}, f32[4,128,128]{2,1,0:T(8,128)S(1)}, u32[]{:S(2)}, u32[]{:S(2)}) collective-permute-start(f32[4,128,128]{2,1,0:T(8,128)S(1)} %select_add_fusion.4), channel_id=1, source_target_pairs={{0,32},{8,40},{16,48},{24,56},{32,64},{40,72},{48,80},{56,88},{64,... | collective-permute-start | bytes 786440 | tf_op jit(solution)/shard_map/ppermute | solution.py:283
  326.7 1.3 collective-permute-start.17
  328.6 1.8 collective-permute-done.6
  330.5 7.0 %collective-permute-start.8 = (f32[4,128,128]{2,1,0:T(8,128)S(1)}, f32[4,128,128]{2,1,0:T(8,128)}, u32[]{:S(2)}, u32[]{:S(2)}) collective-permute-start(f32[4,128,128]{2,1,0:T(8,128)S(1)} %select_add_fusion.3), channel_id=1, source_target_pairs={{0,64},{8,72},{16,80},{24,88},{32,96},{40,104},{48,112},{56,120},{... | collective-permute-start | bytes 786440 | tf_op jit(solution)/shard_map/ppermute | solution.py:283
  338.9 2.0 copy.44
  342.0 2.0 copy.43
  344.0 1.3 fusion.13
  346.4 6.8 %copy.97 = bf16[2,288,6144]{2,1,0:T(8,128)(2,1)} copy(bf16[2,288,6144]{2,1,0:T(8,128)(2,1)} %get-tuple-element.26) | data formatting | bytes 14155776
  (61 shorter events, 11.6 us)
Async XLA Ops:
  0.6 8.5 %copy-start = (bf16[512,512]{1,0:T(8,128)(2,1)S(1)}, bf16[512,512]{1,0:T(8,128)(2,1)}, u32[]{:S(2)}) copy-start(bf16[512,512]{1,0:T(8,128)(2,1)} %param.13) | copy-start | bytes 1572868
  3.2 271.7 %collective-permute-start.10 = (f32[4]{0:T(128)S(1)}, f32[4]{0:T(128)S(1)}, u32[]{:S(2)}, u32[]{:S(2)}) collective-permute-start(f32[4]{0:T(128)S(1)} %bitcast_exponential_fusion), channel_id=1, source_target_pairs={{8,0},{16,8},{24,16},{32,24},{40,32},{48,40},{56,48},{64,56},{72,6... | collective-permute-start | bytes 56 | tf_op jit(solution)/shard_map/ppermute | solution.py:283
  4.5 271.8 %collective-permute-start.1 = (f32[4]{0:T(128)S(1)}, f32[4]{0:T(128)S(1)}, u32[]{:S(2)}, u32[]{:S(2)}) collective-permute-start(f32[4]{0:T(128)S(1)} %bitcast_exponential_fusion), channel_id=1, source_target_pairs={{0,8},{8,16},{16,24},{24,32},{32,40},{40,48},{48,56},{56,64},{64,7... | collective-permute-start | bytes 56 | tf_op jit(solution)/shard_map/ppermute | solution.py:283
  11.7 280.6 %collective-permute-start = (f32[4,128,128]{2,1,0:T(8,128)}, f32[4,128,128]{2,1,0:T(8,128)S(1)}, u32[]{:S(2)}, u32[]{:S(2)}) collective-permute-start(f32[4,128,128]{2,1,0:T(8,128)} %fusion.15), channel_id=1, source_target_pairs={{0,8},{8,16},{16,24},{24,32},{32,40},{40,48},{48,56},{56,64},{64,7... | collective-permute-start | bytes 786440 | tf_op jit(solution)/shard_map/ppermute | solution.py:283
  266.0 16.8 %collective-permute-start.9 = (f32[4,128,128]{2,1,0:T(8,128)S(1)}, f32[4,128,128]{2,1,0:T(8,128)}, u32[]{:S(2)}, u32[]{:S(2)}) collective-permute-start(f32[4,128,128]{2,1,0:T(8,128)S(1)} %fusion.16), channel_id=1, source_target_pairs={{8,0},{16,8},{24,16},{32,24},{40,32},{48,40},{56,48},{64,56},{72,6... | collective-permute-start | bytes 786440 | tf_op jit(solution)/shard_map/ppermute | solution.py:283
  271.3 2.9 copy-start.2
  274.1 63.6 %copy-start.3 = (f32[512,4,128]{0,2,1:T(8,128)S(1)}, f32[512,4,128]{0,2,1:T(8,128)}, u32[]{:S(2)}) copy-start(f32[512,4,128]{0,2,1:T(8,128)} %fusion.1) | copy-start | bytes 3145732
  275.0 6.5 %collective-permute-start.12 = (f32[4]{0:T(128)S(1)}, f32[4]{0:T(128)S(1)}, u32[]{:S(2)}, u32[]{:S(2)}) collective-permute-start(f32[4]{0:T(128)S(1)} %broadcast_select_fusion.3), channel_id=1, source_target_pairs={{8,0},{16,8},{24,16},{32,24},{40,32},{48,40},{56,48},{64,56},{72,6... | collective-permute-start | bytes 56 | tf_op jit(solution)/shard_map/ppermute | solution.py:283
  276.3 7.8 %collective-permute-start.3 = (f32[4]{0:T(128)S(1)}, f32[4]{0:T(128)S(1)}, u32[]{:S(2)}, u32[]{:S(2)}) collective-permute-start(f32[4]{0:T(128)S(1)} %broadcast_select_fusion.7), channel_id=1, source_target_pairs={{0,8},{8,16},{16,24},{24,32},{32,40},{40,48},{48,56},{56,64},{64,7... | collective-permute-start | bytes 56 | tf_op jit(solution)/shard_map/ppermute | solution.py:283
  281.5 9.3 %collective-permute-start.14 = (f32[4]{0:T(128)S(1)}, f32[4]{0:T(128)S(1)}, u32[]{:S(2)}, u32[]{:S(2)}) collective-permute-start(f32[4]{0:T(128)S(1)} %fusion.34), channel_id=1, source_target_pairs={{16,0},{24,8},{32,16},{40,24},{48,32},{56,40},{64,48},{72,56},{80,... | collective-permute-start | bytes 56 | tf_op jit(solution)/shard_map/ppermute | solution.py:283
  282.8 13.4 %collective-permute-start.11 = (f32[4,128,128]{2,1,0:T(8,128)}, f32[4,128,128]{2,1,0:T(8,128)S(1)}, u32[]{:S(2)}, u32[]{:S(2)}) collective-permute-start(f32[4,128,128]{2,1,0:T(8,128)} %collective-permute-done.9), channel_id=1, source_target_pairs={{8,0},{16,8},{24,16},{32,24},{40,32},{48,40},{56,48},{64,56},{72,6... | collective-permute-start | bytes 786440 | tf_op jit(solution)/shard_map/ppermute | solution.py:283
  284.1 14.5 %collective-permute-start.5 = (f32[4]{0:T(128)S(1)}, f32[4]{0:T(128)S(1)}, u32[]{:S(2)}, u32[]{:S(2)}) collective-permute-start(f32[4]{0:T(128)S(1)} %fusion.31), channel_id=1, source_target_pairs={{0,16},{8,24},{16,32},{24,40},{32,48},{40,56},{48,64},{56,72},{64,... | collective-permute-start | bytes 56 | tf_op jit(solution)/shard_map/ppermute | solution.py:283
  290.9 50.0 %copy-start.1 = (f32[512,4,128]{0,2,1:T(8,128)S(1)}, f32[512,4,128]{0,2,1:T(8,128)}, u32[]{:S(2)}) copy-start(f32[512,4,128]{0,2,1:T(8,128)} %convolution_bitcast_fusion) | copy-start | bytes 3145732
  290.9 26.5 %collective-permute-start.16 = (f32[4]{0:T(128)S(1)}, f32[4]{0:T(128)S(1)}, u32[]{:S(2)}, u32[]{:S(2)}) collective-permute-start(f32[4]{0:T(128)S(1)} %fusion.35), channel_id=1, source_target_pairs={{32,0},{40,8},{48,16},{56,24},{64,32},{72,40},{80,48},{88,56},{96,... | collective-permute-start | bytes 56 | tf_op jit(solution)/shard_map/ppermute | solution.py:283
  292.3 14.3 %collective-permute-start.2 = (f32[4,128,128]{2,1,0:T(8,128)S(1)}, f32[4,128,128]{2,1,0:T(8,128)S(1)}, u32[]{:S(2)}, u32[]{:S(2)}) collective-permute-start(f32[4,128,128]{2,1,0:T(8,128)S(1)} %collective-permute-done), channel_id=1, source_target_pairs={{0,8},{8,16},{16,24},{24,32},{32,40},{40,48},{48,56},{56,64},{64,7... | collective-permute-start | bytes 786440 | tf_op jit(solution)/shard_map/ppermute | solution.py:283
  297.3 18.7 %collective-permute-start.13 = (f32[4,128,128]{2,1,0:T(8,128)S(1)}, f32[4,128,128]{2,1,0:T(8,128)S(1)}, u32[]{:S(2)}, u32[]{:S(2)}) collective-permute-start(f32[4,128,128]{2,1,0:T(8,128)S(1)} %select_add_fusion.2), channel_id=1, source_target_pairs={{16,0},{24,8},{32,16},{40,24},{48,32},{56,40},{64,48},{72,56},{80,... | collective-permute-start | bytes 786440 | tf_op jit(solution)/shard_map/ppermute | solution.py:283
  298.6 29.4 %collective-permute-start.7 = (f32[4]{0:T(128)S(1)}, f32[4]{0:T(128)S(1)}, u32[]{:S(2)}, u32[]{:S(2)}) collective-permute-start(f32[4]{0:T(128)S(1)} %fusion.32), channel_id=1, source_target_pairs={{0,32},{8,40},{16,48},{24,56},{32,64},{40,72},{48,80},{56,88},{64,... | collective-permute-start | bytes 56 | tf_op jit(solution)/shard_map/ppermute | solution.py:283
  306.8 13.1 %collective-permute-start.4 = (f32[4,128,128]{2,1,0:T(8,128)S(1)}, f32[4,128,128]{2,1,0:T(8,128)S(1)}, u32[]{:S(2)}, u32[]{:S(2)}) collective-permute-start(f32[4,128,128]{2,1,0:T(8,128)S(1)} %select_add_fusion.5), channel_id=1, source_target_pairs={{0,16},{8,24},{16,32},{24,40},{32,48},{40,56},{48,64},{56,72},{64,... | collective-permute-start | bytes 786440 | tf_op jit(solution)/shard_map/ppermute | solution.py:283
  316.1 10.5 %collective-permute-start.15 = (f32[4,128,128]{2,1,0:T(8,128)S(1)}, f32[4,128,128]{2,1,0:T(8,128)S(1)}, u32[]{:S(2)}, u32[]{:S(2)}) collective-permute-start(f32[4,128,128]{2,1,0:T(8,128)S(1)} %select_add_fusion.1), channel_id=1, source_target_pairs={{32,0},{40,8},{48,16},{56,24},{64,32},{72,40},{80,48},{88,56},{96,... | collective-permute-start | bytes 786440 | tf_op jit(solution)/shard_map/ppermute | solution.py:283
  319.9 10.5 %collective-permute-start.6 = (f32[4,128,128]{2,1,0:T(8,128)S(1)}, f32[4,128,128]{2,1,0:T(8,128)S(1)}, u32[]{:S(2)}, u32[]{:S(2)}) collective-permute-start(f32[4,128,128]{2,1,0:T(8,128)S(1)} %select_add_fusion.4), channel_id=1, source_target_pairs={{0,32},{8,40},{16,48},{24,56},{32,64},{40,72},{48,80},{56,88},{64,... | collective-permute-start | bytes 786440 | tf_op jit(solution)/shard_map/ppermute | solution.py:283
  326.7 10.9 %collective-permute-start.17 = (f32[4,128,128]{2,1,0:T(8,128)S(1)}, f32[4,128,128]{2,1,0:T(8,128)S(1)}, u32[]{:S(2)}, u32[]{:S(2)}) collective-permute-start(f32[4,128,128]{2,1,0:T(8,128)S(1)} %select_add_fusion), channel_id=1, source_target_pairs={{64,0},{72,8},{80,16},{88,24},{96,32},{104,40},{112,48},{120,56},{... | collective-permute-start | bytes 786440 | tf_op jit(solution)/shard_map/ppermute | solution.py:283
  330.5 13.5 %collective-permute-start.8 = (f32[4,128,128]{2,1,0:T(8,128)S(1)}, f32[4,128,128]{2,1,0:T(8,128)}, u32[]{:S(2)}, u32[]{:S(2)}) collective-permute-start(f32[4,128,128]{2,1,0:T(8,128)S(1)} %select_add_fusion.3), channel_id=1, source_target_pairs={{0,64},{8,72},{16,80},{24,88},{32,96},{40,104},{48,112},{56,120},{... | collective-permute-start | bytes 786440 | tf_op jit(solution)/shard_map/ppermute | solution.py:283

commit v2 on v1

v2 whole, which is shorter than its diff:
```python
import math

import jax
import jax.numpy as jnp
from jax import lax
from jax.experimental import pallas as pl
from jax.experimental.pallas import tpu as pltpu
from jax.sharding import PartitionSpec as P

HEAD = 128
SEQUENCE = 8192
MOST = 9
ROWS = 144
ZCH = 4
CH = 8
F32, BF16 = jnp.float32, jnp.bfloat16


def split(value):
    high = value.astype(BF16)
    return high, (value - high.astype(F32)).astype(BF16)


def dot2(value, other, dims):
    high, low = split(value)
    dims = (dims, ((), ()))
    return lax.dot_general(high, other, dims, preferred_element_type=F32) + lax.dot_general(
        low, other, dims, preferred_element_type=F32
    )


def layer_kernel(
    up_ref, meta_ref, q_ref, k_ref, v_ref, decay_ref, w_hbm, act_hbm,
    down_hbm, dq_ref, dk_ref, dv_ref,
    G, upbuf, metabuf, wbuf, actbuf, acc, stage, grad, tab, colc, rowc, ybuf, xbuf, carry,
    zsend, zrecv, gsend, grecv, ysend, yrecv, xsend, xrecv, lsem, osem,
):
    s, j = lax.axis_index("seq"), lax.axis_index("exp")
    x, y, z, core = s // 4, s % 4, j // 2, j % 2
    width = up_ref.shape[1]
    zw, gw = width // ZCH, width // CH
    scale = 1.0 / math.sqrt(HEAD * SEQUENCE)

    def plane(xx, yy):
        return {"seq": (xx % 4) * 4 + yy % 4, "exp": j}

    def column(zz, cc):
        return {"seq": s, "exp": (zz % 4) * 2 + cc}

    zup, zdown, mate = column(z + 1, core), column(z + 3, core), column(z, 1 - core)
    barrier = pltpu.get_barrier_semaphore()
    for peer in (plane(x + 1, y), plane(x + 3, y), plane(x, y + 1), plane(x, y + 3), zup, zdown, mate):
        pl.semaphore_signal(barrier, inc=1, device_id=peer, device_id_type=pl.DeviceIdType.MESH)

    own = [pltpu.make_async_copy(meta_ref, metabuf.at[j], lsem.at[2])] + [
        pltpu.make_async_copy(up_ref.at[:, k * zw : (k + 1) * zw], upbuf.at[k, j], lsem.at[3 + k])
        for k in range(ZCH)
    ]
    for copy in own:
        copy.start()
    wcopy = pltpu.make_async_copy(w_hbm, wbuf, lsem.at[0])
    acopy = pltpu.make_async_copy(act_hbm, actbuf, lsem.at[1])
    wcopy.start()
    acopy.start()
    pl.semaphore_wait(barrier, 7)

    sent = []

    def send(src, dst, ssem, rsem, dev):
        copy = pltpu.make_async_remote_copy(
            src_ref=src, dst_ref=dst, send_sem=ssem, recv_sem=rsem,
            device_id=dev, device_id_type=pl.DeviceIdType.MESH,
        )
        copy.start()
        sent.append(copy)

    def arrived(ref, ssem, rsem):
        pltpu.make_async_remote_copy(
            src_ref=ref, dst_ref=ref, send_sem=ssem, recv_sem=rsem,
            device_id=mate, device_id_type=pl.DeviceIdType.MESH,
        ).wait_recv()

    def zslot(item, slot):
        return metabuf.at[slot] if item == ZCH else upbuf.at[item, slot]

    def zsource(item):
        return meta_ref if item == ZCH else up_ref.at[:, item * zw : (item + 1) * zw]

    def zgo(item, n, src, slot, rn, dev):
        send(src, zslot(item, slot), zsend.at[item, n], zrecv.at[item, rn], dev)

    def zwait(item, rn, slot):
        arrived(zslot(item, slot), zsend.at[item, 0], zrecv.at[item, rn])

    def exps(zz, cc):
        return ((zz + 4) % 4) * 2 + cc

    for item in (ZCH, *range(ZCH)):
        zgo(item, 0, zsource(item), j, 0, zup)
        zgo(item, 1, zsource(item), j, 1, zdown)
        zgo(item, 2, zsource(item), j, 3, mate)

    def zforward(item):
        below, above = exps(z - 1, core), exps(z + 1, core)
        zwait(item, 0, below)
        if item % 2 == 0:
            zgo(item, 3, zslot(item, below), below, 2, zup)
        zgo(item, 4, zslot(item, below), below, 4, mate)
        zwait(item, 1, above)
        if item % 2 == 1:
            zgo(item, 3, zslot(item, above), above, 2, zdown)
        zgo(item, 5, zslot(item, above), above, 5, mate)

    def zfinish(item):
        far = exps(z + 2, core)
        zwait(item, 2, far)
        zgo(item, 6, zslot(item, far), far, 6, mate)
        for rn, slot in (
            (3, exps(z, 1 - core)),
            (4, exps(z - 1, 1 - core)),
            (5, exps(z + 1, 1 - core)),
            (6, exps(z + 2, 1 - core)),
        ):
            zwait(item, rn, slot)

    def ring(c):
        if c % 2 == 0:
            return x, y, (lambda d: plane(x + d, y)), (lambda d: plane(x, y + d))
        return y, x, (lambda d: plane(x, y + d)), (lambda d: plane(x + d, y))

    def slab(c, a, b):
        place = b * 4 + (a + 4) % 4
        return tab.at[place] if c > CH else G.at[c, place]

    def group(c, b):
        place = pl.ds(((b + 4) % 4) * 4, 4)
        return tab.at[place] if c > CH else G.at[c, place]

    def ggo(c, n, ref, dev):
        send(ref, ref, gsend.at[c, n], grecv.at[c, n], dev)

    def gwait(c, n, ref):
        arrived(ref, gsend.at[c, n], grecv.at[c, n])

    def turn(c):
        return (c // 2) % 2 == 0

    def stage1(c):
        a, b, na, _ = ring(c)
        ggo(c, 0, slab(c, a, b), na(1))
        ggo(c, 1, slab(c, a, b), na(3))

    def stage2(c):
        a, b, na, _ = ring(c)
        if turn(c):
            gwait(c, 0, slab(c, a - 1, b))
            ggo(c, 2, slab(c, a - 1, b), na(1))
            gwait(c, 1, slab(c, a + 1, b))
        else:
            gwait(c, 1, slab(c, a + 1, b))
            ggo(c, 2, slab(c, a + 1, b), na(3))
            gwait(c, 0, slab(c, a - 1, b))

    def stage3(c):
        a, b, _, nb = ring(c)
        gwait(c, 2, slab(c, a + 2, b))
        ggo(c, 3, group(c, b), nb(1))
        ggo(c, 4, group(c, b), nb(3))

    def stage4(c):
        a, b, _, nb = ring(c)
        if turn(c):
            gwait(c, 3, group(c, b - 1))
            ggo(c, 5, group(c, b - 1), nb(1))
            gwait(c, 4, group(c, b + 1))
        else:
            gwait(c, 4, group(c, b + 1))
            ggo(c, 5, group(c, b + 1), nb(3))
            gwait(c, 3, group(c, b - 1))

    outs = []

    def stage5(c):
        a, b, _, _ = ring(c)
        gwait(c, 5, group(c, b + 2))
        if c > CH:
            return
        if c >= 2:
            outs[c - 2].wait()
        for e in range(2):
            order = [(p % 4) * 4 + p // 4 if c % 2 == 0 else p for p in range(16)]
            rows = jnp.concatenate([G[c, p, e * 72 : (e + 1) * 72, :] for p in order], axis=0)
            stage[c % 2, e] = jnp.dot(actbuf[e], rows, preferred_element_type=F32).astype(BF16)
        out = pltpu.make_async_copy(stage.at[c % 2], down_hbm.at[:, :, c * gw : (c + 1) * gw], osem.at[c % 2])
        out.start()
        outs.append(out)

    def states_out(kind, ref, lo):
        for h in range(4):
            cols = slice(h * HEAD, (h + 1) * HEAD)
            c = colc[h]
            factor = jnp.exp(c[511:512, :] - c) if kind == 0 else jnp.exp(c)
            left = ref[:, cols].astype(F32) * factor
            ybuf[kind, y, h] = dot2(left, lo[:, cols], ((0,), (0,))).astype(BF16)

    def ygo(kind):
        send(ybuf.at[kind, y], ybuf.at[kind, y], ysend.at[kind, 0], yrecv.at[kind, 0], plane(x, y + 1))
        send(ybuf.at[kind, y], ybuf.at[kind, y], ysend.at[kind, 1], yrecv.at[kind, 1], plane(x, y + 3))

    def xgo(kind):
        send(xbuf.at[kind, x], xbuf.at[kind, x], xsend.at[kind, 0], xrecv.at[kind, 0], plane(x + 1, y))
        send(xbuf.at[kind, x], xbuf.at[kind, x], xsend.at[kind, 1], xrecv.at[kind, 1], plane(x + 3, y))

    def pass_on(kind, buf, at, ssem, rsem, up, down):
        below, above = buf.at[kind, (at + 3) % 4], buf.at[kind, (at + 1) % 4]
        arrived(below, ssem.at[kind, 0], rsem.at[kind, 0])
        arrived(above, ssem.at[kind, 1], rsem.at[kind, 1])
        if kind == 0:
            send(below, below, ssem.at[kind, 2], rsem.at[kind, 2], up)
        else:
            send(above, above, ssem.at[kind, 2], rsem.at[kind, 2], down)

    def ypass(kind):
        pass_on(kind, ybuf, y, ysend, yrecv, plane(x, y + 1), plane(x, y + 3))

    def xpass(kind):
        pass_on(kind, xbuf, x, xsend, xrecv, plane(x + 1, y), plane(x + 3, y))

    def far(kind, buf, at, ssem, rsem):
        arrived(buf.at[kind, (at + 2) % 4], ssem.at[kind, 2], rsem.at[kind, 2])

    def span(logs, low, high):
        total = jnp.zeros_like(logs[0])
        for r in range(4):
            total = total + jnp.where((r > low) & (r < high), 1.0, 0.0) * logs[r]
        return jnp.exp(total) * jnp.where(low < high, 1.0, 0.0)

    def row_logs():
        return [tab[x * 4 + r] for r in range(4)]

    def mix(coefs, buf, kind, h):
        return sum(coefs[r][h : h + 1, :] * buf[kind, r, h].astype(F32) for r in range(4))

    def states_row(kind):
        far(kind, ybuf, y, ysend, yrecv)
        logs = row_logs()
        coefs = [span(logs, r, 4) if kind == 0 else span(logs, -1, r) for r in range(4)]
        for h in range(4):
            xbuf[kind, x, h] = mix(coefs, ybuf, kind, h).astype(BF16)

    def states_in(kind):
        far(kind, xbuf, x, xsend, xrecv)
        logs = row_logs()
        whole = [sum(tab[q * 4 + r] for r in range(4)) for q in range(4)]
        if kind == 0:
            near = [span(logs, r, y) for r in range(4)]
            rest = span(logs, -1, y)
            wide = [span(whole, q, x) * rest for q in range(4)]
        else:
            near = [span(logs, y, r) for r in range(4)]
            rest = span(logs, y, 4)
            wide = [span(whole, x, q) * rest for q in range(4)]
        for h in range(4):
            total = mix(near, ybuf, kind, h) + mix(wide, xbuf, kind, h)
            high, low = split(total)
            carry[kind, h, 0] = high
            carry[kind, h, 1] = low

    def attention():
        place_t = lax.broadcasted_iota(jnp.int32, (512, 512), 0)
        place_s = lax.broadcasted_iota(jnp.int32, (512, 512), 1)

        def head(h, _):
            cols = pl.ds(pl.multiple_of(h * HEAD, HEAD), HEAD)
            q, k, v, o = q_ref[:, cols], k_ref[:, cols], v_ref[:, cols], grad[:, cols]
            c = colc[h]
            column_c, row_c = jnp.concatenate([c] * 4, axis=1), rowc[h, 0:1, :]
            spread = column_c - row_c
            weight = jnp.where(place_t >= place_s, jnp.exp(jnp.minimum(spread, 0.0)), 0.0)
            flipped = jnp.where(place_t <= place_s, jnp.exp(jnp.minimum(-spread, 0.0)), 0.0)
            lead, tail = jnp.exp(c), jnp.exp(c[511:512, :] - c)

            def outer(one, two):
                return lax.dot_general(one, two, (((1,), (1,)), ((), ())), preferred_element_type=F32)

            def inner(one, two):
                return jnp.dot(one, two, preferred_element_type=F32)

            dq = dot2(outer(o, v) * weight, k, ((1,), (0,)))
            dq = dq + lead * (outer(o, carry[0, h, 0]) + outer(o, carry[0, h, 1]))
            dq_ref[:, cols] = (scale * dq).astype(BF16)
            dk = dot2(outer(v, o) * flipped, q, ((1,), (0,)))
            dk = dk + tail * (outer(v, carry[1, h, 0]) + outer(v, carry[1, h, 1]))
            dk_ref[:, cols] = (scale * dk).astype(BF16)
            dv = dot2(outer(k, q) * flipped, o, ((1,), (0,)))
            dv = dv + tail * (inner(k, carry[1, h, 0]) + inner(k, carry[1, h, 1]))
            dv_ref[:, cols] = (scale * dv).astype(BF16)
            return 0

        lax.fori_loop(0, 4, head, 0)

    logs = decay_ref[...]
    tab[s] = jnp.broadcast_to(jnp.sum(logs, axis=1, keepdims=True), (8, HEAD))
    low = lax.broadcasted_iota(jnp.int32, (512, 512), 0) >= lax.broadcasted_iota(jnp.int32, (512, 512), 1)
    sums = jnp.where(low, 1.0, 0.0).astype(BF16)
    part, rest = [], logs
    for _ in range(3):
        part.append(rest.astype(BF16))
        rest = rest - part[-1].astype(F32)
    for h in range(4):
        colc[h] = sum(
            lax.dot_general(
                sums, jnp.broadcast_to(p[h : h + 1, :], (HEAD, 512)), (((1,), (1,)), ((), ())),
                preferred_element_type=F32,
            )
            for p in part
        )
        rowc[h] = sum(
            lax.dot_general(
                jnp.broadcast_to(p[h : h + 1, :], (8, 512)), sums, (((1,), (1,)), ((), ())),
                preferred_element_type=F32,
            )
            for p in part
        )
    states_out(0, k_ref, v_ref)
    stage1(CH + 1)
    ygo(0)

    for copy in own:
        copy.wait()
    zforward(ZCH)
    zforward(0)
    zfinish(ZCH)
    row = lax.broadcasted_iota(jnp.int32, (ROWS, 64), 0)
    local = row % 72
    expert = (row // 72 + 2 * j).astype(F32)
    second, want, block_of = row // 72 == 1, (local % MOST).astype(F32), local // MOST
    ahead = lax.broadcasted_iota(jnp.int32, (64, 64), 0) < lax.broadcasted_iota(jnp.int32, (64, 64), 1)
    ahead = jnp.where(ahead, 1.0, 0.0).astype(BF16)
    which = (lax.broadcasted_iota(jnp.int32, (8, 64), 0) + 2 * j).astype(F32)
    picks, gates = [], []
    for t in range(8):
        table = metabuf[t]
        name0, name1 = table[0:1, 0:64], table[1:2, 0:64]
        gate0, gate1 = table[2:3, 0:64], table[3:4, 0:64]
        named = jnp.where((which == name0) | (which == name1), 1.0, 0.0)
        rank = jnp.dot(named.astype(BF16), ahead, preferred_element_type=F32)
        right = (jnp.where(second, rank[1:2, :], rank[0:1, :]) == want) & (block_of == t)
        hit0, hit1 = right & (name0 == expert), right & (name1 == expert)
        picks.append(jnp.where(hit0 | hit1, 1.0, 0.0))
        gates.append(jnp.sum(jnp.where(hit0, gate0, 0.0) + jnp.where(hit1, gate1, 0.0), axis=1, keepdims=True))
    pick = jnp.concatenate(picks, axis=1).astype(BF16)
    gate = sum(gates)

    def select(c):
        k, off = c // (CH // ZCH), (c % (CH // ZCH)) * gw
        tokens = upbuf[k, :, :, off : off + gw].reshape(512, gw)
        a, b, _, _ = ring(c)
        rows = jnp.dot(pick, tokens, preferred_element_type=F32)
        G[c, b * 4 + a] = (rows * gate).astype(BF16)
        part = lax.dot_general(
            tokens, wbuf[:, c * gw : (c + 1) * gw], (((1,), (1,)), ((), ())), preferred_element_type=F32
        )
        if c == 0:
            acc[...] = part
        else:
            acc[...] += part
        stage1(c)

    per = CH // ZCH
    for k in range(ZCH):
        zfinish(k)
        if k + 1 < ZCH:
            zforward(k + 1)
        if k == 0:
            wcopy.wait()
        for c in range(per * k, per * k + per):
            select(c)
        if k == 0:
            stage2(CH + 1)
            stage3(CH + 1)
            ypass(0)
        if k == 1:
            stage2(0), stage2(1), stage3(0), stage3(1)
            stage4(CH + 1)
            states_row(0)
            xgo(0)
        if k == 2:
            stage2(2), stage2(3)
            xpass(0)
        if k == 3:
            stage3(2), stage3(3)
            stage2(4), stage2(5)
    grad[...] = acc[...].astype(BF16)
    states_out(1, q_ref, grad)
    stage2(6), stage2(7)
    ygo(1)
    stage4(0), stage4(1)
    stage3(4), stage3(5)
    ypass(1)
    stage5(CH + 1)
    states_in(0)
    stage4(2), stage4(3)
    stage3(6), stage3(7)
    states_row(1)
    acopy.wait()
    xgo(1)
    stage5(0), stage5(1)
    stage4(4), stage4(5)
    xpass(1)
    stage4(6), stage4(7)
    states_in(1)
    attention()
    for c in range(2, CH):
        stage5(c)
    outs[CH - 2].wait()
    outs[CH - 1].wait()
    for copy in sent:
        copy.wait_send()


def layer(upstream, meta, queries, keys, values, decays, out_weight, activations):
    width = upstream.shape[1]
    gw, zw = width // CH, width // ZCH
    here = pl.BlockSpec(memory_space=pltpu.VMEM)
    there = pl.BlockSpec(memory_space=pl.ANY)
    small = jax.ShapeDtypeStruct((512, 512), BF16)
    return pl.pallas_call(
        layer_kernel,
        out_shape=(jax.ShapeDtypeStruct((2, 288, width), BF16), small, small, small),
        in_specs=[here] * 6 + [there] * 2,
        out_specs=(there, here, here, here),
        scratch_shapes=[
            pltpu.VMEM((CH, 16, ROWS, gw), BF16),
            pltpu.VMEM((ZCH, 8, 64, zw), BF16),
            pltpu.VMEM((8, 8, 128), F32),
            pltpu.VMEM((512, width), BF16),
            pltpu.VMEM((2, 288, 1152), BF16),
            pltpu.VMEM((512, 512), F32),
            pltpu.VMEM((2, 2, 288, gw), BF16),
            pltpu.VMEM((512, 512), BF16),
            pltpu.VMEM((16, 8, HEAD), F32),
            pltpu.VMEM((4, 512, HEAD), F32),
            pltpu.VMEM((4, 8, 512), F32),
            pltpu.VMEM((2, 4, 4, HEAD, HEAD), BF16),
            pltpu.VMEM((2, 4, 4, HEAD, HEAD), BF16),
            pltpu.VMEM((2, 4, 2, HEAD, HEAD), BF16),
            pltpu.SemaphoreType.DMA((ZCH + 1, 7)),
            pltpu.SemaphoreType.DMA((ZCH + 1, 7)),
            pltpu.SemaphoreType.DMA((CH + 2, 6)),
            pltpu.SemaphoreType.DMA((CH + 2, 6)),
            pltpu.SemaphoreType.DMA((2, 3)),
            pltpu.SemaphoreType.DMA((2, 3)),
            pltpu.SemaphoreType.DMA((2, 3)),
            pltpu.SemaphoreType.DMA((2, 3)),
            pltpu.SemaphoreType.DMA((3 + ZCH,)),
            pltpu.SemaphoreType.DMA((2,)),
        ],
        compiler_params=pltpu.CompilerParams(
            collective_id=0, has_side_effects=True, vmem_limit_bytes=64000 * 1024
        ),
        name="layer",
    )(upstream, meta, queries, keys, values, decays, out_weight, activations)


def shards(
    upstream, out_weight, queries, keys, values, log_decay, expert_ids, gate_probs, activations
):
    meta = jnp.concatenate([expert_ids.astype(F32).T, gate_probs.T], axis=0)
    meta = jnp.pad(meta, ((0, 4), (0, 64)))
    decays = jnp.pad(log_decay, ((0, 4), (0, 0)))
    d_down, d_queries, d_keys, d_values = layer(
        upstream, meta, queries, keys, values, decays, out_weight, activations
    )
    return (d_queries, d_keys, d_values, d_down)


def solution(mesh):
    return jax.shard_map(
        shards,
        mesh=mesh,
        in_specs=(
            P(("seq", "exp"), None),
            P("exp", None),
            P("seq", "exp"),
            P("seq", "exp"),
            P("seq", "exp"),
            P("exp", "seq"),
            P(("seq", "exp"), None),
            P(("seq", "exp"), None),
            P("exp", "seq", None),
        ),
        out_specs=(P("seq", "exp"), P("seq", "exp"), P("seq", "exp"), P("exp", "seq", None)),
        check_vma=False,
    )
```

time: 355 us -> 220 us (0.62)
  starting transfers between devices: 66.5 us -> 0 us
  Pallas kernels: 244 us -> 203 us
  matrix products: 14.2 us -> 0 us
  waiting for transfers between devices: 4.31 us -> 0 us
  other arithmetic: 5.9 us -> 1.96 us
    ppermute x18 -> x0, starting transfers between devices: 66.5 us -> none  [shift(): return lax.ppermute(part, 'seq', pairs)]
    pallas_call x1, Pallas kernels: 244 us -> 203 us  [layer(): pl.pallas_call(layer_kernel, out_shape=(jax.ShapeDtypeStruct((2, 288, wid...]
    dot_general x10 -> x0, matrix products: 14.2 us -> none  [the longest x9 14.1 us: dot(): return jnp.einsum(spec, a, b, preferred_element_type=F32)]
    ppermute x18 -> x0, waiting for transfers between devices: 4.31 us -> none  [shift(): return lax.ppermute(part, 'seq', pairs)]
    unnamed x15 -> x4, local copies, waits for them, and re-layouts: 12.8 us -> 12.4 us
  transfers between devices with their start and end apart: 18 -> 0, of which waited for: 2 -> 0; matrix products, arithmetic and copies ran while one was open for 7% -> 0% of each run, Pallas kernels for 69% -> 0%
where the time goes in v2:
time: 220 us
  Pallas kernels  203 us (92%)
  local copies, waits for them, and re-layouts  13.7 us (6%)
    pallas_call x1, Pallas kernels, layer(): pl.pallas_call(layer_kernel, out_shape=(jax.ShapeDtypeStruct((2, 288, wid...  203 us
    unnamed x4, local copies, waits for them, and re-layouts  12.4 us

profile of v2, /device:TPU:0, one launch (start us, length us, event | category | flops | bytes accessed | tf_op | source)
XLA Modules:
  0.0 219.6 jit_solution(10233399307625825245)
XLA Ops:
  0.6 0.7 convert_bitcast_fusion
  1.3 1.3 select_maximum_fusion.meta_ref
  2.6 1.3 pad.9.decay_ref
  3.9 203.2 %layer.1 = (bf16[2,288,6144]{2,1,0:T(8,128)(2,1)}, bf16[512,512]{1,0:T(8,128)(2,1)}, bf16[512,512]{1,0:T(8,128)(2,1)}, bf16[512,512]{1,0:T(8,128)(2,1)}) custom-call(bf16[64,6144]{1,0:T(8,128)(2,1)} %up_ref.1, f32[8,128]{1,0:T(8,128)} %select_maximum_fusion.meta_ref, bf16[512,512]{1,0:T(8,128)(2,1)} %q_ref.1, bf16[512,512]{1,0:T(8,128)(2,1)} %k_ref.1, ...), custom_call_target="tpu_custom_call" | custom-call | tf_op jit(solution)/shard_map/layer/pallas_call | solution.py:428
  207.1 1.9 copy.17
  209.0 1.9 copy.18
  210.9 1.9 copy.19
  212.8 6.8 %copy.20 = bf16[2,288,6144]{2,1,0:T(8,128)(2,1)} copy(bf16[2,288,6144]{2,1,0:T(8,128)(2,1)} %get-tuple-element.19) | data formatting | bytes 14155776
